TPU v7x, 32 devices: a whole 2x2x4 slice. The times are simulated.
32 devices in a mesh: seq: 8 (over y, x, core), batch: 4 (over z).
Axes of the slice: x: 2, y: 2, z: 4, core: 2. Of those that a mesh axis runs over, the one named last changes fastest.
Arguments:
- queries: bfloat16 [16, 4096], P('batch', 'seq'), may hold values from -210 to 210
- key_cache: bfloat16 [16, 1024, 2048], P('batch', 'seq'), may hold values from -6 to 6
- value_cache: bfloat16 [16, 1024, 2048], P('batch', 'seq'), may hold values from -12 to 12
- new_key: bfloat16 [16, 2048], P('batch'), may hold values from -6 to 6
- new_value: bfloat16 [16, 2048], P('batch'), may hold values from -12 to 12
- page_table: int32 [16, 8], P('batch', 'seq'), may hold values from 0 to 3, as said below
- counts: int32 [16, 8], P('batch', 'seq'), may hold values from 1 to 128
- offsets: int32 [16], P('batch'), may hold values from 0 to 896
- w_out: bfloat16 [4096, 4608], P('seq', 'batch'), may hold values from -0.09375 to 0.09375
Outputs:
- projected: bfloat16 [16, 4608], P('seq', 'batch')
Inputs may be any that keep to these rules, and one draw needn't show every extreme that they name: `page_table`: for each group of 4 requests and each index along seq, the slots of that index's 1 pages of the group's requests are all different.
All inputs are finite; a program needn't handle non-finite values.
Results may differ from a plain program's by a relative error of at most 0.005.
Values may be sent and summed in bfloat16 or wider, within the bound.
A program may use at most 64 MiB of HBM per device.

v0:
```python
import jax
import jax.numpy as jnp
from jax import lax
from jax.sharding import PartitionSpec as P

HEADS = 32
KVH = 16
HD = 128
QSCALAR = 144
floor_score = -1e30


def joined(x, axis, combine):
    everything = jax.tree.map(lambda part: lax.all_gather(part, axis), x)
    initial = jax.tree.map(lambda part: part[0], everything)

    def turn(k, so_far):
        return combine(so_far, jax.tree.map(lambda part: part[k], everything))

    return lax.fori_loop(1, lax.axis_size(axis), turn, initial)


def on_device(
    queries, key_cache, value_cache, new_key, new_value, page_table, counts, offsets, w_out
):
    requests = queries.shape[0]
    groups = HEADS // KVH
    cycle_size = lax.axis_size("seq")
    cycle_place = lax.axis_index("seq")
    head_count = HEADS // cycle_size
    pages_here = page_table.shape[1]
    page_len = key_cache.shape[1]
    score_multiplier = QSCALAR ** (-0.5)

    def own_heads(array_in):
        return lax.dynamic_slice_in_dim(array_in, cycle_place * head_count, head_count, 1)

    all_queries = lax.all_gather(queries, "seq", axis=1, tiled=True)
    query_lattice = all_queries.reshape(requests, KVH, groups, HD)
    key_rows = jnp.take(key_cache, page_table, axis=0).reshape(
        requests, pages_here * page_len, KVH, HD
    )
    value_rows = jnp.take(value_cache, page_table, axis=0).reshape(
        requests, pages_here * page_len, KVH, HD
    )
    scores = (
        jnp.einsum("bkgd,btkd->bkgt", query_lattice, key_rows, preferred_element_type=jnp.float32)
        * score_multiplier
    )
    token_index = jnp.arange(page_len, dtype=jnp.int32)
    page_start = (cycle_place * pages_here + jnp.arange(pages_here, dtype=jnp.int32)) * page_len
    live_mask = (token_index[None, None, :] < counts[:, :, None]) & (
        page_start[None, :, None] + token_index[None, None, :] >= offsets[:, None, None]
    )
    live_mask = live_mask.reshape(requests, pages_here * page_len)[:, None, None, :]
    peak_score = jnp.max(jnp.where(live_mask, scores, floor_score), axis=-1)
    weights = jnp.where(live_mask, jnp.exp(scores - peak_score[..., None]), 0.0)
    block_total = jnp.sum(weights, axis=-1)
    block_sum = jnp.einsum(
        "bkgt,btkd->bkgd",
        weights.astype(jnp.bfloat16),
        value_rows,
        preferred_element_type=jnp.float32,
    )
    incoming_score = (
        jnp.einsum(
            "pcoz,pcz->pco",
            query_lattice,
            new_key.reshape(requests, KVH, HD),
            preferred_element_type=jnp.float32,
        )
        * score_multiplier
    )
    fresh_value = jnp.broadcast_to(
        new_value.astype(jnp.float32).reshape(requests, KVH, 1, HD), (requests, KVH, groups, HD)
    ).reshape(requests, HEADS, HD)
    flat_peak = peak_score.reshape(requests, HEADS)
    flat_total = block_total.reshape(requests, HEADS)
    flat_sum = block_sum.reshape(requests, HEADS, HD)
    flat_new = incoming_score.reshape(requests, HEADS)
    mine_new = own_heads(flat_new)
    mine_value = own_heads(fresh_value)

    def combine(earlier, later):
        top_score = jnp.maximum(earlier[0], later[0])
        left_weight = jnp.exp(earlier[0] - top_score)
        trailing_weight = jnp.exp(later[0] - top_score)
        return (
            top_score,
            earlier[1] * left_weight + later[1] * trailing_weight,
            earlier[2] * left_weight[..., None] + later[2] * trailing_weight[..., None],
        )

    merged_peak, merged_total, merged_sum = joined(
        (flat_peak, flat_total, flat_sum), "seq", combine
    )
    head_peak = own_heads(merged_peak)
    top_score = jnp.maximum(head_peak, mine_new)
    factor = jnp.exp(head_peak - top_score)
    own_weight = jnp.exp(mine_new - top_score)
    denominator = own_heads(merged_total) * factor + own_weight
    numerator = own_heads(merged_sum) * factor[..., None] + own_weight[..., None] * mine_value
    attention = (
        (numerator / denominator[..., None]).astype(jnp.bfloat16).reshape(requests, head_count * HD)
    )
    everyone = lax.all_gather(attention, "batch", axis=0, tiled=True)
    projected = lax.psum_scatter(
        jnp.dot(everyone, w_out, preferred_element_type=jnp.float32),
        "seq",
        scatter_dimension=0,
        tiled=True,
    )
    return projected.astype(jnp.bfloat16)


def solution(mesh):
    placed = (
        P("batch", "seq"),
        P("batch", "seq", None),
        P("batch", "seq", None),
        P("batch", None),
        P("batch", None),
        P("batch", "seq"),
        P("batch", "seq"),
        P("batch"),
        P("seq", "batch"),
    )
    return jax.shard_map(
        on_device, mesh=mesh, in_specs=placed, out_specs=P("seq", "batch"), check_vma=False
    )
```

profile of v0, /device:TPU:0, one launch (start us, length us, event | category | flops | bytes accessed | tf_op | source)
XLA Modules:
  0.0 98.0 jit_solution(6286090056575001631)
XLA Ops:
  0.0 0.0 copy-start
  0.0 0.8 fusion.15
  0.8 0.8 copy-done
  1.6 2.0 %gather_fusion = bf16[4,128,2048]{2,1,0:T(8,128)(2,1)} fusion(bf16[4,128,2048]{2,1,0:T(8,128)(2,1)S(1)} %copy-done, s32[1024]{0:T(1024)S(1)} %pad_clamp_fusion), kind=kCustom, calls=%fused_computation.clone | custom fusion | bytes 4194320 | tf_op jit(solution)/shard_map/jit(_take)/gather | solution.py:40
  3.6 3.6 %gather_fusion.1 = bf16[4,128,2048]{2,1,0:T(8,128)(2,1)} fusion(bf16[4,128,2048]{2,1,0:T(8,128)(2,1)} %param.15, s32[1024]{0:T(1024)S(1)} %pad_clamp_fusion), kind=kCustom, calls=%fused_computation.1.clone | custom fusion | bytes 4194320 | tf_op jit(solution)/shard_map/jit(_take)/gather | solution.py:43
  7.2 0.0 copy-done.7
  7.2 4.0 %bitcast_select_fusion = (bf16[4,1,128,2048]{3,2,0,1:T(8,128)(2,1)}, bf16[4,1,128,2048]{3,2,0,1:T(8,128)(2,1)S(1)}) fusion(bf16[4,128,2048]{2,1,0:T(8,128)(2,1)} %gather_fusion.1, pred[4]{0:T(512)(128)(4,1)S(1)} %and_bitcast_fusion, bf16[4,128,2048]{2,1,0:T(8,128)(2,1)} %gather_fusion), kind=kLoop, calls=%fused_computation.10 | loop fusion | flops 2097152 | bytes 8388612 | tf_op jit(solution)/shard_map/jit(_take)/select_n | solution.py:43
  11.2 2.0 %copy.35 = bf16[64,8,16,128]{3,2,1,0:T(8,128)(2,1)} copy(bf16[64,8,16,128]{3,1,2,0:T(8,128)(2,1)S(1)} %bitcast.71) | data formatting | bytes 4194304
  13.2 0.0 copy-done.5
  13.2 0.0 copy-done.6
  13.2 0.1 fusion.13
  13.3 10.6 %all_gather.15 = bf16[4,4096]{1,0:T(4,128)(2,1)S(1)} all-gather(bf16[4,512]{1,0:T(4,128)(2,1)S(1)} %copy-done.4), channel_id=1, replica_groups=mesh['seq'=8,'batch'=4] {'seq'}, dimensions={1}, use_global_device_ids=true | all-gather | bytes 36864 | tf_op jit(solution)/shard_map/all_gather | solution.py:38
  23.9 3.0 %select_reduce_fusion = (f32[4,16,2]{2,1,0:T(8,128)S(1)}, f32[4,16,128,2]{2,3,1,0:T(2,128)S(1)}) fusion(pred[4,128]{1,0:T(4,128)(4,1)S(1)} %fusion.13, bf16[4,16,2,128]{3,2,1,0:T(2,128)(2,1)S(1)} %reshape.104, bf16[4,128,16,128]{3,2,1,0:T(8,128)(2,1)} %bitcast.72), kind=kOutput, calls=%fused_computation.21 | convolution fusion | flops 4243328 | bytes 2196480 | tf_op jit(solution)/shard_map/bkgd,btkd->bkgt/dot_general | solution.py:47
  26.9 0.6 copy.36
  27.5 0.0 copy-start.2
  27.6 0.0 copy-start.3
  27.6 0.7 fusion.3
  28.3 9.8 %all_gather.18 = f32[8,4,32,128]{3,2,1,0:T(8,128)S(1)} all-gather(f32[1,4,32,128]{3,2,1,0:T(8,128)S(1)} %bitcast.76), channel_id=1, replica_groups=mesh['seq'=8,'batch'=4] {'seq'}, dimensions={0}, use_global_device_ids=true | all-gather | bytes 589824 | tf_op jit(solution)/shard_map/all_gather | solution.py:14
  38.1 0.3 bitcast_reduce_fusion
  38.4 0.2 copy.25
  38.6 0.1 copy.26
  38.7 7.9 %all_gather.17 = f32[8,4,32]{2,1,0:T(4,128)S(1)} all-gather(f32[1,4,32]{2,1,0:T(4,128)S(1)} %copy.26), channel_id=1, replica_groups=mesh['seq'=8,'batch'=4] {'seq'}, dimensions={0}, use_global_device_ids=true | all-gather | bytes 4608 | tf_op jit(solution)/shard_map/all_gather | solution.py:14
  46.6 0.2 copy.23
  46.8 0.1 copy.24
  46.9 8.9 %all_gather.16 = f32[8,4,32]{2,1,0:T(4,128)S(1)} all-gather(f32[1,4,32]{2,1,0:T(4,128)S(1)} %copy.24), channel_id=1, replica_groups=mesh['seq'=8,'batch'=4] {'seq'}, dimensions={0}, use_global_device_ids=true | all-gather | bytes 4608 | tf_op jit(solution)/shard_map/all_gather | solution.py:14
  55.8 1.1 %while.19 = (s32[]{:T(128)}, f32[4,32]{1,0:T(4,128)S(1)}, f32[4,32]{1,0:T(4,128)S(1)}, f32[4,32,128]{2,1,0:T(8,128)S(1)}, f32[8,4,32]{2,1,0:T(4,128)S(1)}, /*ind...) while((s32[]{:T(128)}, f32[4,32]{1,0:T(4,128)S(1)}, ...), condition=%wide.region_3.5_spmd, body=%wide.region_2.4_spmd.sunk | while | flops 49925 | bytes 201879 | solution.py:20
  55.8 0.1 fusion.29
  56.0 0.1 fusion.29
  56.1 0.1 fusion.29
  56.3 0.1 fusion.29
  56.5 0.1 fusion.29
  56.6 0.1 fusion.29
  56.8 0.1 fusion.29
  56.9 0.1 copy.28
  57.0 0.1 copy.31
  57.1 0.0 copy-done.2
  57.1 0.2 fusion.19
  57.3 0.2 copy.34
  57.6 0.1 copy.29
  57.7 0.1 copy.30
  57.8 0.1 copy.32
  57.9 0.1 fusion.10
  58.0 13.4 %all-gather = bf16[4,4,512]{2,1,0:T(4,128)(2,1)S(1)} all-gather(bf16[1,4,512]{2,1,0:T(4,128)(2,1)S(1)} %reshape.129), channel_id=1, replica_groups=mesh['seq'=8,'batch'=4] {'batch'}, dimensions={0}, use_global_device_ids=true | all-gather | bytes 20480 | tf_op jit(solution)/shard_map/all_gather | solution.py:106
  71.5 1.5 %fusion.20 = f32[16,1152]{1,0:T(8,128)S(1)} fusion(bf16[16,512]{1,0:T(8,128)(2,1)S(1)} %reshape.130, bf16[512,1152]{1,0:T(8,128)(2,1)} %param.21), kind=kOutput, calls=%fused_computation.44 | convolution fusion | flops 18874368 | bytes 1269760 | tf_op jit(solution)/shard_map/dot_general | solution.py:108
  73.0 23.1 %all-reduce = bf16[16,1152]{1,0:T(8,128)(2,1)S(1)} all-reduce(f32[16,1152]{1,0:T(8,128)S(1)} %fusion.20), channel_id=2, replica_groups=mesh['seq'=8,'batch'=4] {'seq'}, use_global_device_ids=true, to_apply=%region_4.6.clone | all-reduce | flops 18432 | bytes 110592
  96.1 0.0 copy-done.8
  96.1 0.6 dynamic-slice
  97.4 0.6 dynamic-slice_convert_fusion
  (31 shorter events, 0.4 us)
Async XLA Ops:
  0.0 1.6 %copy-start = (bf16[4,128,2048]{2,1,0:T(8,128)(2,1)S(1)}, bf16[4,128,2048]{2,1,0:T(8,128)(2,1)}, u32[]{:S(2)}) copy-start(bf16[4,128,2048]{2,1,0:T(8,128)(2,1)} %param.14) | copy-start | bytes 6291460
  3.6 3.6 %copy-start.7 = (s32[4,1]{0,1:T(1,128)S(1)}, s32[4,1]{0,1:T(1,128)}, u32[]{:S(2)}) copy-start(s32[4,1]{0,1:T(1,128)} %param.18) | copy-start | bytes 52
  11.2 2.0 %copy-start.5 = (s32[4,1]{0,1:T(1,128)S(1)}, s32[4,1]{0,1:T(1,128)}, u32[]{:S(2)}) copy-start(s32[4,1]{0,1:T(1,128)} %param.19) | copy-start | bytes 52
  11.2 2.0 %copy-start.6 = (s32[4]{0:T(128)S(1)}, s32[4]{0:T(128)}, u32[]{:S(2)}) copy-start(s32[4]{0:T(128)} %param.20) | copy-start | bytes 52
  11.2 2.1 %copy-start.4 = (bf16[4,512]{1,0:T(4,128)(2,1)S(1)}, bf16[4,512]{1,0:T(4,128)(2,1)}, u32[]{:S(2)}) copy-start(bf16[4,512]{1,0:T(4,128)(2,1)} %param.13) | copy-start | bytes 12292
  23.9 3.0 %copy-start.1 = (bf16[4,1,128,2048]{3,2,0,1:T(8,128)(2,1)S(1)}, bf16[4,1,128,2048]{3,2,0,1:T(8,128)(2,1)}, u32[]{:S(2)}) copy-start(bf16[4,1,128,2048]{3,2,0,1:T(8,128)(2,1)} %get-tuple-element.215) | copy-start | bytes 6291460
  27.5 29.5 %copy-start.2 = (bf16[4,2048]{1,0:T(4,128)(2,1)S(1)}, bf16[4,2048]{1,0:T(4,128)(2,1)}, u32[]{:S(2)}) copy-start(bf16[4,2048]{1,0:T(4,128)(2,1)} %param.16) | copy-start | bytes 49156
  27.6 30.3 %copy-start.3 = (bf16[4,2048]{1,0:T(4,128)(2,1)S(1)}, bf16[4,2048]{1,0:T(4,128)(2,1)}, u32[]{:S(2)}) copy-start(bf16[4,2048]{1,0:T(4,128)(2,1)} %param.17) | copy-start | bytes 49156
  38.1 58.0 %copy-start.8 = (u32[32]{0:T(128)S(1)}, u32[32]{0:T(128)}, u32[]{:S(2)}) copy-start(u32[32]{0:T(128)} %constant.74) | copy-start | bytes 388
where the time goes:
time: 98.3 us; the launch traced here: 98 us
  blocking collectives  73.8 us (75%)
  local copies, waits for them, and re-layouts  11.6 us (12%)
  other arithmetic  6.21 us (6%)
  matrix products  5.44 us (6%)
    all_gather x3, blocking collectives, joined(): everything = jax.tree.map(lambda part: lax.all_gather(part, axis), x)  26.6 us
    unnamed x1, blocking collectives  23.1 us
    all_gather x1, blocking collectives, on_device(): everyone = lax.all_gather(attention, 'batch', axis=0, tiled=True)  13.4 us
    all_gather x1, blocking collectives, on_device(): all_queries = lax.all_gather(queries, 'seq', axis=1, tiled=True)  10.6 us
    unnamed x24, local copies, waits for them, and re-layouts  4.04 us
    select_n x1, other arithmetic, on_device(): jnp.take(value_cache, page_table, axis=0)  3.96 us
    gather x1, local copies, waits for them, and re-layouts, on_device(): jnp.take(value_cache, page_table, axis=0)  3.58 us
    dot_general x1, matrix products, on_device(): jnp.einsum('bkgd,btkd->bkgt', query_lattice, key_rows, preferred_element_...  3.01 us

commit v1 on v0

--- a/solution.py
+++ b/solution.py
@@ -35,7 +35,7 @@
     def own_heads(array_in):
         return lax.dynamic_slice_in_dim(array_in, cycle_place * head_count, head_count, 1)
 
-    all_queries = lax.all_gather(queries, "seq", axis=1, tiled=True)
+    all_queries = jnp.concatenate(lax.all_gather(queries, "seq"), axis=1)
     query_lattice = all_queries.reshape(requests, KVH, groups, HD)
     key_rows = jnp.take(key_cache, page_table, axis=0).reshape(
         requests, pages_here * page_len, KVH, HD

time: 98.3 us -> 98.3 us (level)
  no operation moved by 1% of the time
where the time goes in v1:
time: 98.3 us; the launch traced here: 98 us
  blocking collectives  73.8 us (75%)
  local copies, waits for them, and re-layouts  11.6 us (12%)
  other arithmetic  6.21 us (6%)
  matrix products  5.44 us (6%)
    all_gather x3, blocking collectives, joined(): everything = jax.tree.map(lambda part: lax.all_gather(part, axis), x)  26.6 us
    unnamed x1, blocking collectives  23.1 us
    all_gather x1, blocking collectives, on_device(): everyone = lax.all_gather(attention, 'batch', axis=0, tiled=True)  13.4 us
    all_gather x1, blocking collectives, on_device(): all_queries = jnp.concatenate(lax.all_gather(queries, 'seq'), axis=1)  10.6 us
    unnamed x24, local copies, waits for them, and re-layouts  4.04 us
    select_n x1, other arithmetic, on_device(): jnp.take(value_cache, page_table, axis=0)  3.96 us
    gather x1, local copies, waits for them, and re-layouts, on_device(): jnp.take(value_cache, page_table, axis=0)  3.58 us
    dot_general x1, matrix products, on_device(): jnp.einsum('bkgd,btkd->bkgt', query_lattice, key_rows, preferred_element_...  3.01 us

profile of v1, /device:TPU:0, one launch (start us, length us, event | category | flops | bytes accessed | tf_op | source)
XLA Modules:
  0.0 98.0 jit_solution(1977995981467387669)
XLA Ops:
  0.0 0.0 copy-start
  0.0 0.8 fusion.15
  0.8 0.8 copy-done
  1.6 2.0 %gather_fusion = bf16[4,128,2048]{2,1,0:T(8,128)(2,1)} fusion(bf16[4,128,2048]{2,1,0:T(8,128)(2,1)S(1)} %copy-done, s32[1024]{0:T(1024)S(1)} %pad_clamp_fusion), kind=kCustom, calls=%fused_computation.clone | custom fusion | bytes 4194320 | tf_op jit(solution)/shard_map/jit(_take)/gather | solution.py:40
  3.6 3.6 %gather_fusion.1 = bf16[4,128,2048]{2,1,0:T(8,128)(2,1)} fusion(bf16[4,128,2048]{2,1,0:T(8,128)(2,1)} %param.15, s32[1024]{0:T(1024)S(1)} %pad_clamp_fusion), kind=kCustom, calls=%fused_computation.1.clone | custom fusion | bytes 4194320 | tf_op jit(solution)/shard_map/jit(_take)/gather | solution.py:43
  7.2 0.0 copy-done.7
  7.2 4.0 %bitcast_select_fusion = (bf16[4,1,128,2048]{3,2,0,1:T(8,128)(2,1)}, bf16[4,1,128,2048]{3,2,0,1:T(8,128)(2,1)S(1)}) fusion(bf16[4,128,2048]{2,1,0:T(8,128)(2,1)} %gather_fusion.1, pred[4]{0:T(512)(128)(4,1)S(1)} %and_bitcast_fusion, bf16[4,128,2048]{2,1,0:T(8,128)(2,1)} %gather_fusion), kind=kLoop, calls=%fused_computation.10 | loop fusion | flops 2097152 | bytes 8388612 | tf_op jit(solution)/shard_map/jit(_take)/select_n | solution.py:43
  11.2 2.0 %copy.37 = bf16[64,8,16,128]{3,2,1,0:T(8,128)(2,1)} copy(bf16[64,8,16,128]{3,1,2,0:T(8,128)(2,1)S(1)} %bitcast.73) | data formatting | bytes 4194304
  13.2 0.0 copy-done.5
  13.2 0.0 copy-done.6
  13.2 0.1 fusion.13
  13.2 0.0 copy-done.4
  13.3 10.6 %all-gather.1 = bf16[8,4,512]{2,1,0:T(4,128)(2,1)S(1)} all-gather(bf16[1,4,512]{2,1,0:T(4,128)(2,1)S(1)} %bitcast.83), channel_id=2, replica_groups=mesh['seq'=8,'batch'=4] {'seq'}, dimensions={0}, use_global_device_ids=true | all-gather | bytes 36864 | tf_op jit(solution)/shard_map/all_gather | solution.py:38
  23.9 3.0 %select_reduce_fusion = (f32[4,16,2]{2,1,0:T(8,128)S(1)}, f32[4,16,128,2]{2,3,1,0:T(2,128)S(1)}) fusion(pred[4,128]{1,0:T(4,128)(4,1)S(1)} %fusion.13, bf16[4,16,2,128]{3,2,1,0:T(2,128)(2,1)S(1)} %reshape_reshape.3, bf16[4,128,16,128]{3,2,1,0:T(8,128)(2,1)} %bitcast.74), kind=kOutput, calls=%fused_computation.21 | convolution fusion | flops 4243328 | bytes 2196480 | tf_op jit(solution)/shard_map/bkgd,btkd->bkgt/dot_general | solution.py:47
  26.9 0.0 copy-done.1
  26.9 0.6 copy.38
  27.5 0.0 copy-start.2
  27.5 0.0 copy-start.3
  27.6 0.7 fusion.3
  28.3 9.8 %all_gather.22 = f32[8,4,32,128]{3,2,1,0:T(8,128)S(1)} all-gather(f32[1,4,32,128]{3,2,1,0:T(8,128)S(1)} %bitcast.79), channel_id=1, replica_groups=mesh['seq'=8,'batch'=4] {'seq'}, dimensions={0}, use_global_device_ids=true | all-gather | bytes 589824 | tf_op jit(solution)/shard_map/all_gather | solution.py:14
  38.1 0.3 bitcast_reduce_fusion
  38.4 0.2 copy.27
  38.6 0.1 copy.28
  38.6 7.9 %all_gather.21 = f32[8,4,32]{2,1,0:T(4,128)S(1)} all-gather(f32[1,4,32]{2,1,0:T(4,128)S(1)} %copy.28), channel_id=1, replica_groups=mesh['seq'=8,'batch'=4] {'seq'}, dimensions={0}, use_global_device_ids=true | all-gather | bytes 4608 | tf_op jit(solution)/shard_map/all_gather | solution.py:14
  46.6 0.2 copy.25
  46.8 0.1 copy.26
  46.9 8.9 %all_gather.20 = f32[8,4,32]{2,1,0:T(4,128)S(1)} all-gather(f32[1,4,32]{2,1,0:T(4,128)S(1)} %copy.26), channel_id=1, replica_groups=mesh['seq'=8,'batch'=4] {'seq'}, dimensions={0}, use_global_device_ids=true | all-gather | bytes 4608 | tf_op jit(solution)/shard_map/all_gather | solution.py:14
  55.8 1.1 %while.19 = (s32[]{:T(128)}, f32[4,32]{1,0:T(4,128)S(1)}, f32[4,32]{1,0:T(4,128)S(1)}, f32[4,32,128]{2,1,0:T(8,128)S(1)}, f32[8,4,32]{2,1,0:T(4,128)S(1)}, /*ind...) while((s32[]{:T(128)}, f32[4,32]{1,0:T(4,128)S(1)}, ...), condition=%wide.region_3.5_spmd, body=%wide.region_2.4_spmd.sunk | while | flops 49925 | bytes 201879 | solution.py:20
  55.8 0.1 fusion.29
  55.9 0.1 fusion.29
  56.1 0.1 fusion.29
  56.3 0.1 fusion.29
  56.4 0.1 fusion.29
  56.6 0.1 fusion.29
  56.8 0.1 fusion.29
  56.9 0.1 copy.30
  57.0 0.1 copy.33
  57.1 0.2 fusion.19
  57.3 0.2 copy.36
  57.6 0.1 copy.31
  57.7 0.1 copy.32
  57.8 0.1 copy.34
  57.9 0.1 fusion.10
  58.0 13.4 %all-gather.2 = bf16[4,4,512]{2,1,0:T(4,128)(2,1)S(1)} all-gather(bf16[1,4,512]{2,1,0:T(4,128)(2,1)S(1)} %reshape.132), channel_id=1, replica_groups=mesh['seq'=8,'batch'=4] {'batch'}, dimensions={0}, use_global_device_ids=true | all-gather | bytes 20480 | tf_op jit(solution)/shard_map/all_gather | solution.py:106
  71.5 1.5 %fusion.20 = f32[16,1152]{1,0:T(8,128)S(1)} fusion(bf16[16,512]{1,0:T(8,128)(2,1)S(1)} %reshape.133, bf16[512,1152]{1,0:T(8,128)(2,1)} %param.21), kind=kOutput, calls=%fused_computation.44 | convolution fusion | flops 18874368 | bytes 1269760 | tf_op jit(solution)/shard_map/dot_general | solution.py:108
  73.0 23.1 %all-reduce = bf16[16,1152]{1,0:T(8,128)(2,1)S(1)} all-reduce(f32[16,1152]{1,0:T(8,128)S(1)} %fusion.20), channel_id=3, replica_groups=mesh['seq'=8,'batch'=4] {'seq'}, use_global_device_ids=true, to_apply=%region_4.6.clone | all-reduce | flops 18432 | bytes 110592
  96.1 0.6 dynamic-slice
  97.4 0.6 dynamic-slice_convert_fusion
  (32 shorter events, 0.4 us)
Async XLA Ops:
  0.0 1.6 %copy-start = (bf16[4,128,2048]{2,1,0:T(8,128)(2,1)S(1)}, bf16[4,128,2048]{2,1,0:T(8,128)(2,1)}, u32[]{:S(2)}) copy-start(bf16[4,128,2048]{2,1,0:T(8,128)(2,1)} %param.14) | copy-start | bytes 6291460
  3.6 3.6 %copy-start.7 = (s32[4,1]{0,1:T(1,128)S(1)}, s32[4,1]{0,1:T(1,128)}, u32[]{:S(2)}) copy-start(s32[4,1]{0,1:T(1,128)} %param.18) | copy-start | bytes 52
  11.2 2.0 %copy-start.5 = (s32[4,1]{0,1:T(1,128)S(1)}, s32[4,1]{0,1:T(1,128)}, u32[]{:S(2)}) copy-start(s32[4,1]{0,1:T(1,128)} %param.19) | copy-start | bytes 52
  11.2 2.0 %copy-start.6 = (s32[4]{0:T(128)S(1)}, s32[4]{0:T(128)}, u32[]{:S(2)}) copy-start(s32[4]{0:T(128)} %param.20) | copy-start | bytes 52
  11.2 2.1 %copy-start.4 = (bf16[4,512]{1,0:T(4,128)(2,1)S(1)}, bf16[4,512]{1,0:T(4,128)(2,1)}, u32[]{:S(2)}) copy-start(bf16[4,512]{1,0:T(4,128)(2,1)} %param.13) | copy-start | bytes 12292
  23.9 3.0 %copy-start.1 = (bf16[4,1,128,2048]{3,2,0,1:T(8,128)(2,1)S(1)}, bf16[4,1,128,2048]{3,2,0,1:T(8,128)(2,1)}, u32[]{:S(2)}) copy-start(bf16[4,1,128,2048]{3,2,0,1:T(8,128)(2,1)} %get-tuple-element.215) | copy-start | bytes 6291460
  27.5 29.5 %copy-start.2 = (bf16[4,2048]{1,0:T(4,128)(2,1)S(1)}, bf16[4,2048]{1,0:T(4,128)(2,1)}, u32[]{:S(2)}) copy-start(bf16[4,2048]{1,0:T(4,128)(2,1)} %param.16) | copy-start | bytes 49156
  27.5 30.3 %copy-start.3 = (bf16[4,2048]{1,0:T(4,128)(2,1)S(1)}, bf16[4,2048]{1,0:T(4,128)(2,1)}, u32[]{:S(2)}) copy-start(bf16[4,2048]{1,0:T(4,128)(2,1)} %param.17) | copy-start | bytes 49156
  38.1 58.0 %copy-start.8 = (u32[32]{0:T(128)S(1)}, u32[32]{0:T(128)}, u32[]{:S(2)}) copy-start(u32[32]{0:T(128)} %constant.74) | copy-start | bytes 388
